TPU v7x, 128 devices: a whole 4x4x4 slice. The times are simulated.
128 devices in a mesh: samples: 8 (over y, x_hi), space: 16 (over x_lo, z, core).
Axes of the slice: x: 4 (x_hi: 2, x_lo: 2; x = x_hi * 2 + x_lo), y: 4, z: 4, core: 2. Of those that a mesh axis runs over, the one named last changes fastest.
Arguments:
- target: bfloat16 [8, 16384, 8192], P(None, 'samples', 'space'), may hold values from 0 to 1
- a_factor: bfloat16 [16384, 256], P(('samples', 'space')), may hold values from -3 to 3
- b_factor: bfloat16 [8192, 256], P(('space', 'samples')), may hold values from -3 to 3
- c_factor: bfloat16 [8, 256], replicated, may hold values from -3 to 3
Outputs:
- grad_a: float32 [16384, 256], P(('samples', 'space'))
- grad_b: float32 [8192, 256], P(('space', 'samples'))
- grad_c: float32 [8, 256], replicated
All inputs are finite; a program needn't handle non-finite values.
Results may differ from a plain program's by a relative error of at most 0.002.
Values may be sent and summed in bfloat16 or wider, within the bound.
No kernel may reach another device: no remote copies, remote signals or barrier semaphores. Data moves between devices by JAX's collectives and lax.ppermute only.
A program may use at most 128 MiB of HBM per device.

v0:
```python
import jax
import jax.numpy as jnp
from jax import lax
from jax.sharding import PartitionSpec as P


def on_device(target, a_factor, b_factor, c_factor):
    a_full = lax.all_gather(a_factor, "space", axis=0, tiled=True)
    b_full = lax.all_gather(b_factor, "samples", axis=0, tiled=True)
    c_wide = c_factor.astype(jnp.float32)
    scaled = (c_wide[:, None, :] * a_full.astype(jnp.float32)[None]).astype(jnp.bfloat16)
    model = jnp.einsum("kir,jr->kij", scaled, b_full, preferred_element_type=jnp.float32)
    derivative = (jax.nn.sigmoid(model) - target.astype(jnp.float32)).astype(jnp.bfloat16)
    weighted = jnp.einsum("kij,ir->kjr", derivative, a_full, preferred_element_type=jnp.float32)
    b_part = jnp.sum(weighted * c_wide[:, None, :], axis=0)
    c_part = jnp.sum(weighted * b_full.astype(jnp.float32)[None], axis=1)
    own_a = a_factor.shape[0]
    own_b = b_factor.shape[0]
    inner = jnp.einsum("kij,jr->kir", derivative, b_full, preferred_element_type=jnp.float32)
    whole_a = lax.psum(jnp.sum(inner * c_wide[:, None, :], axis=0), "space")
    grad_a = lax.dynamic_slice_in_dim(whole_a, lax.axis_index("space") * own_a, own_a, 0)
    whole_b = lax.psum(b_part, "samples")
    grad_b = lax.dynamic_slice_in_dim(whole_b, lax.axis_index("samples") * own_b, own_b, 0)
    grad_c = lax.psum(c_part, ("samples", "space"))
    return (grad_a, grad_b, grad_c)


def solution(mesh):
    return jax.shard_map(
        on_device,
        mesh=mesh,
        in_specs=(
            P(None, "samples", "space"),
            P(("samples", "space"), None),
            P(("space", "samples"), None),
            P(),
        ),
        out_specs=(P(("samples", "space"), None), P(("space", "samples"), None), P()),
        check_vma=False,
    )
```

profile of v0, /device:TPU:1, one launch (start us, length us, event | category | flops | bytes accessed | tf_op | source)
XLA Modules:
  0.0 294.9 jit_solution(3848630474228114266)
XLA Ops:
  7.2 0.0 all-gather.2.cloned.1.call-start
  7.2 0.7 all-gather.2.cloned.1.call-update
  7.9 0.0 all-reduce.5.cloned.1.call-start
  7.9 0.7 convert_element_type.18
  8.6 30.6 %all_gather.7 = bf16[512,256]{1,0:T(8,128)(2,1)S(1)} all-gather(bf16[64,256]{1,0:T(8,128)(2,1)} %param.6), channel_id=1, replica_groups=mesh['samples'=8,'space'=16] {'samples'}, dimensions={0}, use_global_device_ids=true | all-gather | bytes 294912 | tf_op jit(solution)/shard_map/all_gather | solution.py:9
  39.3 6.7 %all-gather.2.cloned.1.call-done = bf16[2048,256]{1,0:T(8,128)(2,1)} async-done(((bf16[128,256]{1,0:T(8,128)(2,1)}), bf16[2048,256]{1,0:T(8,128)(2,1)}) %all-gather.2.cloned.1.call-update) | async-done | bytes 1048592 | tf_op jit(solution)/shard_map/all_gather | solution.py:8
  46.0 1.4 convert_element_type.19
  47.4 0.0 copy-start
  47.4 17.1 %subtract_convert_fusion = bf16[8,2048,512]{2,1,0:T(8,128)(2,1)} fusion(bf16[8,2048,512]{2,1,0:T(8,128)(2,1)} %param.4, f32[2048,256]{1,0:T(8,128)S(1)} %convert_element_type.19, f32[8,256]{1,0:T(8,128)S(1)} %convert_element_type.18, bf16[512,256]{1,0:T(8,128)(2,1)S(1)} %all_gather.7), kind=kOutput, calls=%fused_computation | convolution fusion | flops 4353687552 | bytes 35921920 | tf_op jit(solution)/shard_map/kir,jr->kij/dot_general | solution.py:12
  64.4 0.0 copy-done
  64.4 11.7 %multiply_reduce_fusion.1 = (f32[8,256]{1,0:T(8,128)S(1)}, f32[512,256]{1,0:T(8,128)}) fusion(f32[512,256]{1,0:T(8,128)S(1)} %convert_element_type.23, f32[8,256]{1,0:T(8,128)S(1)} %convert_element_type.18, bf16[8,2048,512]{2,1,0:T(8,128)(2,1)} %subtract_convert_fusion, bf16[2048,256]{1,0:T(8,128)(2,1)S(1)} %copy-done), kind=kOutput, calls=%fused_computation.5 | convolution fusion | flops 4299028480 | bytes 18890752 | tf_op jit(solution)/shard_map/kij,ir->kjr/dot_general | solution.py:14
  76.2 0.0 all-reduce.5.cloned.1.call-update
  76.2 0.2 all-reduce.3.cloned.1.call-start
  76.4 11.8 %multiply_reduce_fusion = f32[2048,256]{1,0:T(8,128)} fusion(f32[8,256]{1,0:T(8,128)S(1)} %convert_element_type.18, bf16[8,2048,512]{2,1,0:T(8,128)(2,1)} %subtract_convert_fusion, bf16[512,256]{1,0:T(8,128)(2,1)S(1)} %all_gather.7), kind=kOutput, calls=%fused_computation.1 | convolution fusion | flops 4302831616 | bytes 19144704 | tf_op jit(solution)/shard_map/kij,jr->kir/dot_general | solution.py:19
  88.2 0.0 all-reduce.3.cloned.1.call-update
  88.2 66.9 %psum.23 = f32[8,256]{1,0:T(8,128)} all-reduce(f32[8,256]{1,0:T(8,128)S(1)} %get-tuple-element.3), channel_id=1, replica_groups=mesh['samples'=8,'space'=16] {'samples','space'}, use_global_device_ids=true, to_apply=%region_5.0 | all-reduce | flops 2048 | bytes 16384 | tf_op jit(solution)/shard_map/psum | solution.py:24
  155.1 3.3 %all-reduce.5.cloned.1.call-done = f32[512,256]{1,0:T(8,128)} async-done(((f32[512,256]{1,0:T(8,128)}), f32[512,256]{1,0:T(8,128)}) %all-reduce.5.cloned.1.call-update) | async-done | bytes 524304 | tf_op jit(solution)/shard_map/psum | solution.py:22
  158.5 1.5 constant_dynamic-slice_fusion
  160.0 126.8 %all-reduce.3.cloned.1.call-done = f32[2048,256]{1,0:T(8,128)} async-done(((f32[2048,256]{1,0:T(8,128)}), f32[2048,256]{1,0:T(8,128)}) %all-reduce.3.cloned.1.call-update) | async-done | bytes 2097168 | tf_op jit(solution)/shard_map/psum | solution.py:20
  286.8 1.6 constant_dynamic-slice_fusion.1
  (1 shorter events, 0.0 us)
Async XLA Ops:
  7.2 38.8 %all-gather.2.cloned.1.call-start = ((), (), s32[]{:S(2)}) async-start(), calls=%async_computation | async-start | bytes 1114112 | tf_op jit(solution)/shard_map/all_gather | solution.py:8
  7.9 150.6 %all-reduce.5.cloned.1.call-start = ((), (), s32[]{:S(2)}) async-start(), calls=%async_computation.2 | async-start | bytes 1048576 | tf_op jit(solution)/shard_map/psum | solution.py:22
  47.4 17.1 %copy-start = (bf16[2048,256]{1,0:T(8,128)(2,1)S(1)}, bf16[2048,256]{1,0:T(8,128)(2,1)}, u32[]{:S(2)}) copy-start(bf16[2048,256]{1,0:T(8,128)(2,1)} %all-gather.2.cloned.1.call-done) | copy-start | bytes 3145732
  76.2 210.6 %all-reduce.3.cloned.1.call-start = ((), (), s32[]{:S(2)}) async-start(), calls=%async_computation.1 | async-start | bytes 4194304 | tf_op jit(solution)/shard_map/psum | solution.py:20
Sparse Core Ops, SparseCore 0:
  9.7 36.2 all-gather.1
  76.3 82.1 all-reduce.4
  161.1 125.5 all-reduce.2
where the time goes:
time: 295 us
  waiting for transfers between devices  138 us (47%)
  blocking collectives  97.5 us (33%)
  matrix products  40.6 us (14%)
  between operations  13.8 us (5%)
  local copies, waits for them, and re-layouts  3.04 us (1%)
    psum x1, waiting for transfers between devices, on_device(): whole_a = lax.psum(jnp.sum(inner * c_wide[:, None, :], axis=0), 'space')  127 us
    psum x1, blocking collectives, on_device(): grad_c = lax.psum(c_part, ('samples', 'space'))  66.9 us
    all_gather x1, blocking collectives, on_device(): b_full = lax.all_gather(b_factor, 'samples', axis=0, tiled=True)  30.6 us
    dot_general x1, matrix products, on_device(): jnp.einsum('kir,jr->kij', scaled, b_full, preferred_element_type=jnp.floa...  17.1 us
    dot_general x1, matrix products, on_device(): jnp.einsum('kij,jr->kir', derivative, b_full, preferred_element_type=jnp....  11.8 us
    dot_general x1, matrix products, on_device(): jnp.einsum('kij,ir->kjr', derivative, a_full, preferred_element_type=jnp....  11.7 us
    all_gather x1, waiting for transfers between devices, on_device(): a_full = lax.all_gather(a_factor, 'space', axis=0, tiled=True)  6.71 us
  transfers between devices with their start and end apart: 3, of which 3 were waited for; matrix products, arithmetic and copies ran while one was open for 5% of the time, Pallas kernels for 0%

commit v1 on v0

--- a/solution.py
+++ b/solution.py
@@ -6,7 +6,9 @@
 
 def on_device(target, a_factor, b_factor, c_factor):
     a_full = lax.all_gather(a_factor, "space", axis=0, tiled=True)
-    b_full = lax.all_gather(b_factor, "samples", axis=0, tiled=True)
+    b_full = jnp.concatenate(
+        lax.all_to_all(jnp.stack([b_factor] * lax.axis_size("samples")), "samples", 0, 0), axis=0
+    )
     c_wide = c_factor.astype(jnp.float32)
     scaled = (c_wide[:, None, :] * a_full.astype(jnp.float32)[None]).astype(jnp.bfloat16)
     model = jnp.einsum("kir,jr->kij", scaled, b_full, preferred_element_type=jnp.float32)

time: 295 us -> 294 us (level)
  blocking collectives: 97.5 us -> 66.7 us
  waiting for transfers between devices: 138 us -> 158 us
  starting transfers between devices: 0.3 us -> 7.78 us
    all_gather x1 -> x0, blocking collectives: 30.6 us -> none  [on_device(): b_full = lax.all_gather(b_factor, 'samples', axis=0, tiled=True)]
    all_gather x1, waiting for transfers between devices: 6.71 us -> 21.4 us  [on_device(): a_full = lax.all_gather(a_factor, 'space', axis=0, tiled=True)]
    all_to_all x0 -> x1, starting transfers between devices: none -> 7.48 us  [on_device(): lax.all_to_all(jnp.stack([b_factor] * lax.axis_size('samples')), 'samples...]
    all_to_all x0 -> x1, waiting for transfers between devices: none -> 6.9 us  [on_device(): lax.all_to_all(jnp.stack([b_factor] * lax.axis_size('samples')), 'samples...]
  transfers between devices with their start and end apart: 3 -> 4, of which waited for: 3 -> 4; matrix products, arithmetic and copies ran while one was open for 5% -> 5% of each run, Pallas kernels for 0% -> 0%
where the time goes in v1:
time: 294 us; the launch traced here: 293 us
  waiting for transfers between devices  158 us (54%)
  blocking collectives  66.7 us (23%)
  matrix products  40.6 us (14%)
  between operations  13.8 us (5%)
  starting transfers between devices  7.78 us (3%)
  local copies, waits for them, and re-layouts  4.51 us (2%)
    psum x1, waiting for transfers between devices, on_device(): whole_a = lax.psum(jnp.sum(inner * c_wide[:, None, :], axis=0), 'space')  127 us
    psum x1, blocking collectives, on_device(): grad_c = lax.psum(c_part, ('samples', 'space'))  66.7 us
    all_gather x1, waiting for transfers between devices, on_device(): a_full = lax.all_gather(a_factor, 'space', axis=0, tiled=True)  21.4 us
    dot_general x1, matrix products, on_device(): jnp.einsum('kir,jr->kij', scaled, b_full, preferred_element_type=jnp.floa...  17.1 us
    dot_general x1, matrix products, on_device(): jnp.einsum('kij,jr->kir', derivative, b_full, preferred_element_type=jnp....  11.8 us
    dot_general x1, matrix products, on_device(): jnp.einsum('kij,ir->kjr', derivative, a_full, preferred_element_type=jnp....  11.7 us
    all_to_all x1, starting transfers between devices, on_device(): lax.all_to_all(jnp.stack([b_factor] * lax.axis_size('samples')), 'samples...  7.48 us
    all_to_all x1, waiting for transfers between devices, on_device(): lax.all_to_all(jnp.stack([b_factor] * lax.axis_size('samples')), 'samples...  6.9 us
  transfers between devices with their start and end apart: 4, of which 4 were waited for; matrix products, arithmetic and copies ran while one was open for 5% of the time, Pallas kernels for 0%

profile of v1, /device:TPU:1, one launch (start us, length us, event | category | flops | bytes accessed | tf_op | source)
XLA Modules:
  0.0 293.2 jit_solution(5684274755794992528)
XLA Ops:
  7.2 0.0 all-gather.2.cloned.1.call-start
  7.2 0.7 all-gather.2.cloned.1.call-update
  7.9 1.5 stack.2
  9.4 7.5 %all-to-all-start = ((bf16[8,64,256]{2,1,0:T(8,128)(2,1)}), bf16[8,64,256]{2,1,0:T(8,128)(2,1)S(1)}, u32[]{:S(2)}, u32[]{:S(2)}) async-start(bf16[8,64,256]{2,1,0:T(8,128)(2,1)} %stack.2), calls=%async_computation | async-start | bytes 524288 | tf_op jit(solution)/shard_map/all_to_all | solution.py:10
  16.8 0.0 all-reduce.5.cloned.1.call-start
  16.9 0.7 convert_element_type.22
  17.6 6.9 %all-to-all-done = bf16[8,64,256]{2,1,0:T(8,128)(2,1)S(1)} async-done(((bf16[8,64,256]{2,1,0:T(8,128)(2,1)}), bf16[8,64,256]{2,1,0:T(8,128)(2,1)S(1)}, u32[]{:S(2)}, u32[]{:S(2)}) %all-to-all-start) | async-done | bytes 262176 | tf_op jit(solution)/shard_map/all_to_all | solution.py:10
  24.5 0.1 bitcast_convert_fusion
  24.5 21.4 %all-gather.2.cloned.1.call-done = bf16[2048,256]{1,0:T(8,128)(2,1)} async-done(((bf16[128,256]{1,0:T(8,128)(2,1)}), bf16[2048,256]{1,0:T(8,128)(2,1)}) %all-gather.2.cloned.1.call-update) | async-done | bytes 1048592 | tf_op jit(solution)/shard_map/all_gather | solution.py:8
  45.9 1.4 convert_element_type.23
  47.3 0.0 copy-start
  47.3 17.1 %subtract_convert_fusion = bf16[8,2048,512]{2,1,0:T(8,128)(2,1)} fusion(bf16[8,2048,512]{2,1,0:T(8,128)(2,1)} %param.4, bf16[512,256,1]{1,0,2:T(8,128)(2,1)S(1)} %bitcast.13, f32[2048,256]{1,0:T(8,128)S(1)} %convert_element_type.23, f32[8,256]{1,0:T(8,128)S(1)} %convert_element_type.22), kind=kOutput, calls=%fused_computation | convolution fusion | flops 4353687552 | bytes 35921920 | tf_op jit(solution)/shard_map/kir,jr->kij/dot_general | solution.py:14
  64.4 0.0 copy-done
  64.4 11.7 %multiply_reduce_fusion.1 = (f32[8,256]{1,0:T(8,128)S(1)}, f32[512,256]{1,0:T(8,128)}) fusion(f32[512,256]{1,0:T(8,128)S(1)} %bitcast_convert_fusion, f32[8,256]{1,0:T(8,128)S(1)} %convert_element_type.22, bf16[8,2048,512]{2,1,0:T(8,128)(2,1)} %subtract_convert_fusion, bf16[2048,256]{1,0:T(8,128)(2,1)S(1)} %copy-done), kind=kOutput, calls=%fused_computation.5 | convolution fusion | flops 4299028480 | bytes 18890752 | tf_op jit(solution)/shard_map/kij,ir->kjr/dot_general | solution.py:16
  76.1 0.0 all-reduce.5.cloned.1.call-update
  76.1 0.2 all-reduce.3.cloned.1.call-start
  76.4 11.8 %multiply_reduce_fusion = f32[2048,256]{1,0:T(8,128)} fusion(f32[8,256]{1,0:T(8,128)S(1)} %convert_element_type.22, bf16[8,2048,512]{2,1,0:T(8,128)(2,1)} %subtract_convert_fusion, bf16[512,256,1]{1,0,2:T(8,128)(2,1)S(1)} %bitcast.14), kind=kOutput, calls=%fused_computation.1 | convolution fusion | flops 4302831616 | bytes 19144704 | tf_op jit(solution)/shard_map/kij,jr->kir/dot_general | solution.py:21
  88.2 0.0 all-reduce.3.cloned.1.call-update
  88.2 66.7 %psum.23 = f32[8,256]{1,0:T(8,128)} all-reduce(f32[8,256]{1,0:T(8,128)S(1)} %get-tuple-element.3), channel_id=1, replica_groups=mesh['samples'=8,'space'=16] {'samples','space'}, use_global_device_ids=true, to_apply=%region_5.0 | all-reduce | flops 2048 | bytes 16384 | tf_op jit(solution)/shard_map/psum | solution.py:26
  154.9 2.0 all-reduce.5.cloned.1.call-done
  156.9 1.5 constant_dynamic-slice_fusion
  158.4 126.7 %all-reduce.3.cloned.1.call-done = f32[2048,256]{1,0:T(8,128)} async-done(((f32[2048,256]{1,0:T(8,128)}), f32[2048,256]{1,0:T(8,128)}) %all-reduce.3.cloned.1.call-update) | async-done | bytes 2097168 | tf_op jit(solution)/shard_map/psum | solution.py:22
  285.1 1.6 constant_dynamic-slice_fusion.1
Async XLA Ops:
  7.2 38.8 %all-gather.2.cloned.1.call-start = ((), (), s32[]{:S(2)}) async-start(), calls=%async_computation.1 | async-start | bytes 1114112 | tf_op jit(solution)/shard_map/all_gather | solution.py:8
  9.4 15.1 %all-to-all-start = ((bf16[8,64,256]{2,1,0:T(8,128)(2,1)}), bf16[8,64,256]{2,1,0:T(8,128)(2,1)S(1)}, u32[]{:S(2)}, u32[]{:S(2)}) async-start(bf16[8,64,256]{2,1,0:T(8,128)(2,1)} %stack.2), calls=%async_computation | async-start | bytes 524288 | tf_op jit(solution)/shard_map/all_to_all | solution.py:10
  16.8 140.1 %all-reduce.5.cloned.1.call-start = ((), (), s32[]{:S(2)}) async-start(), calls=%async_computation.3 | async-start | bytes 1048576 | tf_op jit(solution)/shard_map/psum | solution.py:24
  47.3 17.1 %copy-start = (bf16[2048,256]{1,0:T(8,128)(2,1)S(1)}, bf16[2048,256]{1,0:T(8,128)(2,1)}, u32[]{:S(2)}) copy-start(bf16[2048,256]{1,0:T(8,128)(2,1)} %all-gather.2.cloned.1.call-done) | copy-start | bytes 3145732
  76.1 209.0 %all-reduce.3.cloned.1.call-start = ((), (), s32[]{:S(2)}) async-start(), calls=%async_computation.2 | async-start | bytes 4194304 | tf_op jit(solution)/shard_map/psum | solution.py:22
Sparse Core Ops, SparseCore 0:
  9.7 36.1 all-gather.1
  76.3 80.6 all-reduce.4
  159.6 125.4 all-reduce.2

commit v2 on v0

--- a/solution.py
+++ b/solution.py
@@ -17,7 +17,7 @@
     own_a = a_factor.shape[0]
     own_b = b_factor.shape[0]
     inner = jnp.einsum("kij,jr->kir", derivative, b_full, preferred_element_type=jnp.float32)
-    whole_a = lax.psum(jnp.sum(inner * c_wide[:, None, :], axis=0), "space")
+    whole_a = jnp.sum(lax.all_gather(jnp.sum(inner * c_wide[:, None, :], axis=0), "space"), axis=0)
     grad_a = lax.dynamic_slice_in_dim(whole_a, lax.axis_index("space") * own_a, own_a, 0)
     whole_b = lax.psum(b_part, "samples")
     grad_b = lax.dynamic_slice_in_dim(whole_b, lax.axis_index("samples") * own_b, own_b, 0)

time: 295 us -> 354 us (1.20)
  waiting for transfers between devices: 138 us -> 185 us
  other arithmetic: 2.11 us -> 14.2 us
    all_gather x0 -> x1, waiting for transfers between devices: none -> 174 us  [on_device(): lax.all_gather(jnp.sum(inner * c_wide[:, None, :], axis=0), 'space')]
    psum x1 -> x0, waiting for transfers between devices: 127 us -> none  [on_device(): whole_a = lax.psum(jnp.sum(inner * c_wide[:, None, :], axis=0), 'space')]
    reduce_sum x0 -> x1, other arithmetic: none -> 12.1 us  [on_device(): jnp.sum(lax.all_gather(jnp.sum(inner * c_wide[:, None, :], axis=0), 'spac...]
  transfers between devices with their start and end apart: 3 -> 3, of which waited for: 3 -> 3; matrix products, arithmetic and copies ran while one was open for 5% -> 4% of each run, Pallas kernels for 0% -> 0%
where the time goes in v2:
time: 354 us; the launch traced here: 353 us
  waiting for transfers between devices  185 us (52%)
  blocking collectives  97.5 us (28%)
  matrix products  40.5 us (11%)
  other arithmetic  14.2 us (4%)
  between operations  13.8 us (4%)
    all_gather x1, waiting for transfers between devices, on_device(): lax.all_gather(jnp.sum(inner * c_wide[:, None, :], axis=0), 'space')  174 us
    psum x1, blocking collectives, on_device(): grad_c = lax.psum(c_part, ('samples', 'space'))  66.9 us
    all_gather x1, blocking collectives, on_device(): b_full = lax.all_gather(b_factor, 'samples', axis=0, tiled=True)  30.6 us
    dot_general x1, matrix products, on_device(): jnp.einsum('kir,jr->kij', scaled, b_full, preferred_element_type=jnp.floa...  17.1 us
    reduce_sum x1, other arithmetic, on_device(): jnp.sum(lax.all_gather(jnp.sum(inner * c_wide[:, None, :], axis=0), 'spac...  12.1 us
    dot_general x1, matrix products, on_device(): jnp.einsum('kij,jr->kir', derivative, b_full, preferred_element_type=jnp....  11.8 us
    dot_general x1, matrix products, on_device(): jnp.einsum('kij,ir->kjr', derivative, a_full, preferred_element_type=jnp....  11.7 us
  transfers between devices with their start and end apart: 3, of which 3 were waited for; matrix products, arithmetic and copies ran while one was open for 4% of the time, Pallas kernels for 0%

profile of v2, /device:TPU:1, one launch (start us, length us, event | category | flops | bytes accessed | tf_op | source)
XLA Modules:
  0.0 353.4 jit_solution(2482330960223403645)
XLA Ops:
  7.2 0.0 all-gather.4.cloned.1.call-start
  7.2 0.7 all-gather.4.cloned.1.call-update
  7.9 0.0 all-reduce.2.cloned.1.call-start
  7.9 0.7 convert_element_type.18
  8.6 30.6 %all_gather.13 = bf16[512,256]{1,0:T(8,128)(2,1)S(1)} all-gather(bf16[64,256]{1,0:T(8,128)(2,1)} %param.6), channel_id=1, replica_groups=mesh['samples'=8,'space'=16] {'samples'}, dimensions={0}, use_global_device_ids=true | all-gather | bytes 294912 | tf_op jit(solution)/shard_map/all_gather | solution.py:9
  39.3 6.7 %all-gather.4.cloned.1.call-done = bf16[2048,256]{1,0:T(8,128)(2,1)} async-done(((bf16[128,256]{1,0:T(8,128)(2,1)}), bf16[2048,256]{1,0:T(8,128)(2,1)}) %all-gather.4.cloned.1.call-update) | async-done | bytes 1048592 | tf_op jit(solution)/shard_map/all_gather | solution.py:8
  46.0 1.4 convert_element_type.19
  47.4 0.0 copy-start
  47.4 17.1 %subtract_convert_fusion = bf16[8,2048,512]{2,1,0:T(8,128)(2,1)} fusion(bf16[8,2048,512]{2,1,0:T(8,128)(2,1)} %param.4, f32[2048,256]{1,0:T(8,128)S(1)} %convert_element_type.19, f32[8,256]{1,0:T(8,128)S(1)} %convert_element_type.18, bf16[512,256]{1,0:T(8,128)(2,1)S(1)} %all_gather.13), kind=kOutput, calls=%fused_computation | convolution fusion | flops 4353687552 | bytes 35921920 | tf_op jit(solution)/shard_map/kir,jr->kij/dot_general | solution.py:12
  64.4 0.0 copy-done
  64.4 11.7 %multiply_reduce_fusion.1 = (f32[8,256]{1,0:T(8,128)S(1)}, f32[512,256]{1,0:T(8,128)}) fusion(f32[512,256]{1,0:T(8,128)S(1)} %convert_element_type.23, f32[8,256]{1,0:T(8,128)S(1)} %convert_element_type.18, bf16[8,2048,512]{2,1,0:T(8,128)(2,1)} %subtract_convert_fusion, bf16[2048,256]{1,0:T(8,128)(2,1)S(1)} %copy-done), kind=kOutput, calls=%fused_computation.5 | convolution fusion | flops 4299028480 | bytes 18890752 | tf_op jit(solution)/shard_map/kij,ir->kjr/dot_general | solution.py:14
  76.1 0.0 all-reduce.2.cloned.1.call-update
  76.2 0.2 all-gather.6.cloned.1.call-start
  76.4 11.8 %multiply_reduce_fusion = f32[2048,256]{1,0:T(8,128)} fusion(f32[8,256]{1,0:T(8,128)S(1)} %convert_element_type.18, bf16[8,2048,512]{2,1,0:T(8,128)(2,1)} %subtract_convert_fusion, bf16[512,256]{1,0:T(8,128)(2,1)S(1)} %all_gather.13), kind=kOutput, calls=%fused_computation.1 | convolution fusion | flops 4302831616 | bytes 19144704 | tf_op jit(solution)/shard_map/kij,jr->kir/dot_general | solution.py:19
  88.2 0.0 all-gather.6.cloned.1.call-update
  88.2 66.9 %psum.15 = f32[8,256]{1,0:T(8,128)} all-reduce(f32[8,256]{1,0:T(8,128)S(1)} %get-tuple-element.3), channel_id=1, replica_groups=mesh['samples'=8,'space'=16] {'samples','space'}, use_global_device_ids=true, to_apply=%region_5.0 | all-reduce | flops 2048 | bytes 16384 | tf_op jit(solution)/shard_map/psum | solution.py:24
  155.1 3.3 all-reduce.2.cloned.1.call-done
  158.4 1.5 constant_dynamic-slice_fusion
  159.9 174.2 %all-gather.6.cloned.1.call-done = f32[32768,256]{1,0:T(8,128)} async-done(((f32[2048,256]{1,0:T(8,128)}), f32[32768,256]{1,0:T(8,128)}) %all-gather.6.cloned.1.call-update) | async-done | bytes 33554448 | tf_op jit(solution)/shard_map/all_gather | solution.py:20
  334.1 12.1 %reduce_sum.37 = f32[2048,256]{1,0:T(8,128)S(1)} reduce(f32[16,2048,256]{2,1,0:T(8,128)} %bitcast.13, f32[]{:T(128)} %constant.4.clone.1), dimensions={0}, to_apply=%region_1.0 | reduce | flops 7864320 | bytes 35651588 | tf_op jit(solution)/shard_map/reduce_sum | solution.py:20
  346.2 0.7 constant_dynamic-slice_fusion.1
  (1 shorter events, 0.0 us)
Async XLA Ops:
  7.2 38.8 %all-gather.4.cloned.1.call-start = ((), (), s32[]{:S(2)}) async-start(), calls=%async_computation | async-start | bytes 1114112 | tf_op jit(solution)/shard_map/all_gather | solution.py:8
  7.9 150.5 %all-reduce.2.cloned.1.call-start = ((), (), s32[]{:S(2)}) async-start(), calls=%async_computation.1 | async-start | bytes 1048576 | tf_op jit(solution)/shard_map/psum | solution.py:22
  47.4 17.1 %copy-start = (bf16[2048,256]{1,0:T(8,128)(2,1)S(1)}, bf16[2048,256]{1,0:T(8,128)(2,1)}, u32[]{:S(2)}) copy-start(bf16[2048,256]{1,0:T(8,128)(2,1)} %all-gather.4.cloned.1.call-done) | copy-start | bytes 3145732
  76.2 257.9 %all-gather.6.cloned.1.call-start = ((), (), s32[]{:S(2)}) async-start(), calls=%async_computation.2 | async-start | bytes 35651584 | tf_op jit(solution)/shard_map/all_gather | solution.py:20
Sparse Core Ops, SparseCore 0:
  9.7 36.2 all-gather.3
  76.3 82.1 all-reduce.1
  160.3 173.7 all-gather.5
